TPU v7x, 128 devices: a whole 4x4x4 slice. The times are simulated.
128 devices in a mesh: section: 8 (over y, core), seq: 16 (over z, x).
Axes of the slice: x: 4, y: 4, z: 4, core: 2. Of those that a mesh axis runs over, the one named last changes fastest.
Arguments:
- queries: bfloat16 [8, 2, 2048, 4096], P('section', None, 'seq'), may hold values from -20 to 20
- keys_values: bfloat16 [8, 2, 2048, 8, 256], P('section', None, 'seq'), may hold values from -20 to 20
- lengths: int32 [8, 2, 4], P('section'), may hold values from 1 to 1024, 2048 in all within a row
- order: int32 [8, 2], P('section'), may hold values from 0 to 1, each once within a row
Outputs:
- handoff: bfloat16 [8, 2, 2048, 4096], P('section', None, 'seq')
Inputs may be any that keep to these rules, and one draw needn't show every extreme that they name: Each row holds the lengths of 4 documents packed end to end, summing to 2048, the longest exactly 1024. `order`: each row is a permutation of the microbatch numbers.
All inputs are finite; a program needn't handle non-finite values.
Results may differ from a plain program's by a relative error of at most 0.0037.
Values may be sent and summed in bfloat16 or wider, within the bound.
No kernel may reach another device: no remote copies, remote signals or barrier semaphores. Data moves between devices by JAX's collectives and lax.ppermute only.
A program may use at most 64 MiB of HBM per device.

v0:
```python
import jax
import jax.numpy as jnp
from jax import lax
from jax.sharding import PartitionSpec as P

HD = 128
QH = 32
KVH = 8


def shortened(value):
    return jax.tree.map(lambda a: a.astype(jnp.bfloat16) if a.dtype == jnp.float32 else a, value)


def passed_along(block, axis, distance):
    devices = range(lax.axis_size(axis))
    route = [((i - distance) % len(devices), i) for i in devices]
    return lax.ppermute(block, axis, route)


def segment_ids(lengths_row, rows_all):
    ends = jnp.cumsum(lengths_row)
    position = jnp.arange(rows_all, dtype=jnp.int32)
    return jnp.sum((position[:, None] >= ends[None, :]).astype(jnp.int32), axis=1)


def attend(query_rows, pair_rows, lengths_row):
    rows_all = query_rows.shape[0]
    head_count = query_rows.shape[1] // HD
    pair_count = pair_rows.shape[1] // (2 * HD)
    share_count = head_count // pair_count
    scaling = HD ** (-0.5)
    segment = segment_ids(lengths_row, rows_all)
    position = jnp.arange(rows_all, dtype=jnp.int32)
    block_rows = min(512, rows_all)

    def one_block(block_index):
        row_start = block_index * block_rows
        query_block = lax.dynamic_slice_in_dim(query_rows, row_start, block_rows, 0)
        segment_query = lax.dynamic_slice_in_dim(segment, row_start, block_rows, 0)
        position_query = lax.dynamic_slice_in_dim(position, row_start, block_rows, 0)
        allowed = (segment_query[:, None] == segment[None, :]) & (
            position[None, :] <= position_query[:, None]
        )
        results = []
        for head_index in range(head_count):
            pair_head = head_index // share_count
            query_cols = query_block[:, head_index * HD : (head_index + 1) * HD]
            key_cols = pair_rows[:, pair_head * 2 * HD : pair_head * 2 * HD + HD]
            value_cols = pair_rows[:, pair_head * 2 * HD + HD : (pair_head + 1) * 2 * HD]
            scores = (
                lax.dot_general(
                    query_cols,
                    key_cols,
                    (((1,), (1,)), ((), ())),
                    preferred_element_type=jnp.float32,
                )
                * scaling
            )
            peaks = jnp.max(jnp.where(allowed, scores, -jnp.inf), axis=1, keepdims=True)
            weights = jnp.where(allowed, jnp.exp(scores - peaks), jnp.float32(0.0))
            totals = jnp.sum(weights, axis=1, keepdims=True)
            mixed = (
                jnp.dot(
                    weights.astype(jnp.bfloat16), value_cols, preferred_element_type=jnp.float32
                )
                / totals
            )
            results.append(mixed.astype(jnp.bfloat16))
        return jnp.concatenate(results, axis=1)

    blocks = lax.map(one_block, jnp.arange(rows_all // block_rows, dtype=jnp.int32))
    return blocks.reshape(rows_all, head_count * HD)


def reorder(stacked, order_row):
    picked_all = []
    for slot in range(stacked.shape[0]):
        picked = stacked[0]
        picked = jnp.where(order_row[slot] == 1, stacked[1], picked)
        picked_all.append(picked)
    return jnp.stack(picked_all, axis=0)


def local(queries, keys_values, lengths, order):
    n_seq = lax.axis_size("seq")
    micro = queries.shape[1]
    tok_rows = queries.shape[2]
    all_rows = tok_rows * n_seq
    per_device = QH // n_seq
    repeat_count = max(1, n_seq // KVH)
    kv_local = max(1, KVH // n_seq)
    query_split = queries.reshape(micro, tok_rows, n_seq, per_device * HD)
    wide = jnp.repeat(keys_values.reshape(micro, tok_rows, KVH, 2 * HD), repeat_count, axis=2)
    head_queries, head_pairs = (
        lax.all_to_all(query_split, "seq", split_axis=2, concat_axis=1, tiled=True),
        lax.all_to_all(wide, "seq", split_axis=2, concat_axis=1, tiled=True),
    )
    head_queries = head_queries.reshape(micro, all_rows, per_device * HD)
    head_pairs = head_pairs.reshape(micro, all_rows, kv_local * 2 * HD)
    contexts = jnp.stack(
        [
            attend(head_queries[index_mb], head_pairs[index_mb], lengths[0, index_mb])
            for index_mb in range(micro)
        ],
        axis=0,
    )
    contexts = contexts.reshape(micro, all_rows, 1, per_device * HD)
    back = lax.all_to_all(
        shortened(contexts), "seq", split_axis=1, concat_axis=2, tiled=True
    ).astype(contexts.dtype)
    result = passed_along(shortened(reorder(back, order[0])), "section", 1)
    return result.reshape(1, micro, tok_rows, QH * HD)


def solution(mesh):
    placed = (
        P("section", None, "seq", None),
        P("section", None, "seq", None, None),
        P("section", None, None),
        P("section", None),
    )
    return jax.shard_map(
        local,
        mesh=mesh,
        in_specs=placed,
        out_specs=P("section", None, "seq", None),
        check_vma=False,
    )
```

profile of v0, /device:TPU:0, one launch (start us, length us, event | category | flops | bytes accessed | tf_op | source)
XLA Modules:
  0.0 293.3 jit_solution(14216556808177884193)
XLA Ops:
  5.7 8.0 %all-to-all-start = ((bf16[2,128,16,256]{3,1,0,2:T(8,128)(2,1)}), bf16[2,128,16,256]{3,1,0,2:T(8,128)(2,1)S(1)}, u32[]{:S(2)}, u32[]{:S(2)}) async-start(bf16[2,128,16,256]{3,1,0,2:T(8,128)(2,1)} %copy.46), calls=%async_computation | async-start | bytes 4194304 | tf_op jit(solution)/shard_map/all_to_all | solution.py:96
  15.2 30.3 %all-to-all-done = bf16[2,128,16,256]{3,1,0,2:T(8,128)(2,1)S(1)} async-done(((bf16[2,128,16,256]{3,1,0,2:T(8,128)(2,1)}), bf16[2,128,16,256]{3,1,0,2:T(8,128)(2,1)S(1)}, u32[]{:S(2)}, u32[]{:S(2)}) %all-to-all-start) | async-done | bytes 2097184 | tf_op jit(solution)/shard_map/all_to_all | solution.py:96
  47.1 4.4 %all-to-all-start.1 = ((bf16[2,128,16,256]{3,1,0,2:T(8,128)(2,1)}), bf16[2,128,16,256]{3,1,0,2:T(8,128)(2,1)}, u32[]{:S(2)}, u32[]{:S(2)}) async-start(bf16[2,128,16,256]{3,1,0,2:T(8,128)(2,1)} %bitcast.62), calls=%async_computation.1 | async-start | bytes 4194304 | tf_op jit(solution)/shard_map/all_to_all | solution.py:97
  53.6 27.9 %all-to-all-done.1 = bf16[2,128,16,256]{3,1,0,2:T(8,128)(2,1)} async-done(((bf16[2,128,16,256]{3,1,0,2:T(8,128)(2,1)}), bf16[2,128,16,256]{3,1,0,2:T(8,128)(2,1)}, u32[]{:S(2)}, u32[]{:S(2)}) %all-to-all-start.1) | async-done | bytes 2097184 | tf_op jit(solution)/shard_map/all_to_all | solution.py:97
  84.3 59.1 %while.22 = (s32[]{:T(128)}, bf16[4,512,256]{2,1,0:T(8,128)(2,1)S(1)}, s32[4]{0:T(128)S(1)}, s32[2048]{0:T(1024)S(1)}, s32[2048]{0:T(1024)S(1)}, /*index=5*/bf16...) while((s32[]{:T(128)}, ...), condition=%wide.region_7.8_spmd.clone, body=%wide.region_2.7_spmd.clone.sunk | while | flops 1113323520 | bytes 46268652 | solution.py:72
  85.8 3.8 %select_reduce_fusion.6 = (f32[512]{0:T(512)S(1)}, f32[512,2048]{1,0:T(8,128)}) fusion(s32[512]{0:T(512)S(1)} %dynamic_slice.40, s32[2048]{0:T(1024)S(1)} %get-tuple-element.339, s32[2048]{0:T(1024)S(1)} %get-tuple-element.338, s32[512]{0:T(512)S(1)} %dynamic_slice.41, bf16[2048,256]{1,0:T(8,128)(2,1)S(1)} %get-tuple-element.341, ...), kind=kOutput, calls=%fused_computation.3.clone.1 | convolution fusion | flops 274726400 | bytes 4872196 | tf_op jit(solution)/shard_map/while/body/eval_jaxpr/dot_general | solution.py:52
  89.6 4.6 %fusion.91 = (f32[512]{0:T(512)S(1)}, f32[512]{0:T(512)S(1)}, f32[512,2048]{1,0:T(8,128)S(1)}) fusion(f32[512,2048]{1,0:T(8,128)} %get-tuple-element.258, f32[512]{0:T(512)S(1)} %get-tuple-element.259, s32[512]{0:T(512)S(1)} %dynamic_slice.40, s32[2048]{0:T(1024)S(1)} %get-tuple-element.339, s32[2048]{0:T(1024)S(1)} %get-tuple-element.338, ...), kind=kOutput, calls=%fused_computation.5.clone.1 | convolution fusion | flops 278920192 | bytes 9070600 | tf_op jit(solution)/shard_map/while/body/eval_jaxpr/dot_general | solution.py:52
  104.4 4.6 %fusion.91 = (f32[512]{0:T(512)S(1)}, f32[512]{0:T(512)S(1)}, f32[512,2048]{1,0:T(8,128)S(1)}) fusion(f32[512,2048]{1,0:T(8,128)} %get-tuple-element.258, f32[512]{0:T(512)S(1)} %get-tuple-element.259, s32[512]{0:T(512)S(1)} %dynamic_slice.40, s32[2048]{0:T(1024)S(1)} %get-tuple-element.339, s32[2048]{0:T(1024)S(1)} %get-tuple-element.338, ...), kind=kOutput, calls=%fused_computation.5.clone.1 | convolution fusion | flops 278920192 | bytes 9070600 | tf_op jit(solution)/shard_map/while/body/eval_jaxpr/dot_general | solution.py:52
  115.3 3.8 %select_reduce_fusion.6 = (f32[512]{0:T(512)S(1)}, f32[512,2048]{1,0:T(8,128)}) fusion(s32[512]{0:T(512)S(1)} %dynamic_slice.40, s32[2048]{0:T(1024)S(1)} %get-tuple-element.339, s32[2048]{0:T(1024)S(1)} %get-tuple-element.338, s32[512]{0:T(512)S(1)} %dynamic_slice.41, bf16[2048,256]{1,0:T(8,128)(2,1)S(1)} %get-tuple-element.341, ...), kind=kOutput, calls=%fused_computation.3.clone.1 | convolution fusion | flops 274726400 | bytes 4872196 | tf_op jit(solution)/shard_map/while/body/eval_jaxpr/dot_general | solution.py:52
  119.2 4.6 %fusion.91 = (f32[512]{0:T(512)S(1)}, f32[512]{0:T(512)S(1)}, f32[512,2048]{1,0:T(8,128)S(1)}) fusion(f32[512,2048]{1,0:T(8,128)} %get-tuple-element.258, f32[512]{0:T(512)S(1)} %get-tuple-element.259, s32[512]{0:T(512)S(1)} %dynamic_slice.40, s32[2048]{0:T(1024)S(1)} %get-tuple-element.339, s32[2048]{0:T(1024)S(1)} %get-tuple-element.338, ...), kind=kOutput, calls=%fused_computation.5.clone.1 | convolution fusion | flops 278920192 | bytes 9070600 | tf_op jit(solution)/shard_map/while/body/eval_jaxpr/dot_general | solution.py:52
  130.1 3.8 %select_reduce_fusion.6 = (f32[512]{0:T(512)S(1)}, f32[512,2048]{1,0:T(8,128)}) fusion(s32[512]{0:T(512)S(1)} %dynamic_slice.40, s32[2048]{0:T(1024)S(1)} %get-tuple-element.339, s32[2048]{0:T(1024)S(1)} %get-tuple-element.338, s32[512]{0:T(512)S(1)} %dynamic_slice.41, bf16[2048,256]{1,0:T(8,128)(2,1)S(1)} %get-tuple-element.341, ...), kind=kOutput, calls=%fused_computation.3.clone.1 | convolution fusion | flops 274726400 | bytes 4872196 | tf_op jit(solution)/shard_map/while/body/eval_jaxpr/dot_general | solution.py:52
  133.9 4.6 %fusion.91 = (f32[512]{0:T(512)S(1)}, f32[512]{0:T(512)S(1)}, f32[512,2048]{1,0:T(8,128)S(1)}) fusion(f32[512,2048]{1,0:T(8,128)} %get-tuple-element.258, f32[512]{0:T(512)S(1)} %get-tuple-element.259, s32[512]{0:T(512)S(1)} %dynamic_slice.40, s32[2048]{0:T(1024)S(1)} %get-tuple-element.339, s32[2048]{0:T(1024)S(1)} %get-tuple-element.338, ...), kind=kOutput, calls=%fused_computation.5.clone.1 | convolution fusion | flops 278920192 | bytes 9070600 | tf_op jit(solution)/shard_map/while/body/eval_jaxpr/dot_general | solution.py:52
  143.5 68.4 %while.23 = (s32[]{:T(128)}, bf16[4,512,256]{2,1,0:T(8,128)(2,1)S(1)}, s32[4]{0:T(128)S(1)}, s32[2048]{0:T(1024)S(1)}, s32[2048]{0:T(1024)S(1)}, /*index=5*/bf16...) while((s32[]{:T(128)}, ...), condition=%wide.region_15.16_spmd.clone, body=%wide.region_10.15_spmd.clone.sunk | while | flops 1113323520 | bytes 46268652 | solution.py:72
  145.1 4.0 %select_reduce_fusion.7 = (f32[512]{0:T(512)S(1)}, f32[512,2048]{1,0:T(8,128)}) fusion(s32[512]{0:T(512)S(1)} %dynamic_slice.43, s32[2048]{0:T(1024)S(1)} %get-tuple-element.303, s32[2048]{0:T(1024)S(1)} %get-tuple-element.302, s32[512]{0:T(512)S(1)} %dynamic_slice.44, bf16[2048,256]{1,0:T(8,128)(2,1)} %get-tuple-element.305, ...), kind=kOutput, calls=%fused_computation.33.clone.1 | convolution fusion | flops 274726400 | bytes 4872196 | tf_op jit(solution)/shard_map/while/body/eval_jaxpr/dot_general | solution.py:52
  149.1 4.7 %fusion.99 = (f32[512]{0:T(512)S(1)}, f32[512]{0:T(512)S(1)}, f32[512,2048]{1,0:T(8,128)S(1)}) fusion(f32[512,2048]{1,0:T(8,128)} %get-tuple-element.270, f32[512]{0:T(512)S(1)} %get-tuple-element.271, s32[512]{0:T(512)S(1)} %dynamic_slice.43, s32[2048]{0:T(1024)S(1)} %get-tuple-element.303, s32[2048]{0:T(1024)S(1)} %get-tuple-element.302, ...), kind=kOutput, calls=%fused_computation.35.clone.1 | convolution fusion | flops 278920192 | bytes 9070600 | tf_op jit(solution)/shard_map/while/body/eval_jaxpr/dot_general | solution.py:52
  162.1 4.0 %select_reduce_fusion.7 = (f32[512]{0:T(512)S(1)}, f32[512,2048]{1,0:T(8,128)}) fusion(s32[512]{0:T(512)S(1)} %dynamic_slice.43, s32[2048]{0:T(1024)S(1)} %get-tuple-element.303, s32[2048]{0:T(1024)S(1)} %get-tuple-element.302, s32[512]{0:T(512)S(1)} %dynamic_slice.44, bf16[2048,256]{1,0:T(8,128)(2,1)} %get-tuple-element.305, ...), kind=kOutput, calls=%fused_computation.33.clone.1 | convolution fusion | flops 274726400 | bytes 4872196 | tf_op jit(solution)/shard_map/while/body/eval_jaxpr/dot_general | solution.py:52
  166.1 4.7 %fusion.99 = (f32[512]{0:T(512)S(1)}, f32[512]{0:T(512)S(1)}, f32[512,2048]{1,0:T(8,128)S(1)}) fusion(f32[512,2048]{1,0:T(8,128)} %get-tuple-element.270, f32[512]{0:T(512)S(1)} %get-tuple-element.271, s32[512]{0:T(512)S(1)} %dynamic_slice.43, s32[2048]{0:T(1024)S(1)} %get-tuple-element.303, s32[2048]{0:T(1024)S(1)} %get-tuple-element.302, ...), kind=kOutput, calls=%fused_computation.35.clone.1 | convolution fusion | flops 278920192 | bytes 9070600 | tf_op jit(solution)/shard_map/while/body/eval_jaxpr/dot_general | solution.py:52
  179.2 4.0 %select_reduce_fusion.7 = (f32[512]{0:T(512)S(1)}, f32[512,2048]{1,0:T(8,128)}) fusion(s32[512]{0:T(512)S(1)} %dynamic_slice.43, s32[2048]{0:T(1024)S(1)} %get-tuple-element.303, s32[2048]{0:T(1024)S(1)} %get-tuple-element.302, s32[512]{0:T(512)S(1)} %dynamic_slice.44, bf16[2048,256]{1,0:T(8,128)(2,1)} %get-tuple-element.305, ...), kind=kOutput, calls=%fused_computation.33.clone.1 | convolution fusion | flops 274726400 | bytes 4872196 | tf_op jit(solution)/shard_map/while/body/eval_jaxpr/dot_general | solution.py:52
  183.2 4.7 %fusion.99 = (f32[512]{0:T(512)S(1)}, f32[512]{0:T(512)S(1)}, f32[512,2048]{1,0:T(8,128)S(1)}) fusion(f32[512,2048]{1,0:T(8,128)} %get-tuple-element.270, f32[512]{0:T(512)S(1)} %get-tuple-element.271, s32[512]{0:T(512)S(1)} %dynamic_slice.43, s32[2048]{0:T(1024)S(1)} %get-tuple-element.303, s32[2048]{0:T(1024)S(1)} %get-tuple-element.302, ...), kind=kOutput, calls=%fused_computation.35.clone.1 | convolution fusion | flops 278920192 | bytes 9070600 | tf_op jit(solution)/shard_map/while/body/eval_jaxpr/dot_general | solution.py:52
  196.2 4.0 %select_reduce_fusion.7 = (f32[512]{0:T(512)S(1)}, f32[512,2048]{1,0:T(8,128)}) fusion(s32[512]{0:T(512)S(1)} %dynamic_slice.43, s32[2048]{0:T(1024)S(1)} %get-tuple-element.303, s32[2048]{0:T(1024)S(1)} %get-tuple-element.302, s32[512]{0:T(512)S(1)} %dynamic_slice.44, bf16[2048,256]{1,0:T(8,128)(2,1)} %get-tuple-element.305, ...), kind=kOutput, calls=%fused_computation.33.clone.1 | convolution fusion | flops 274726400 | bytes 4872196 | tf_op jit(solution)/shard_map/while/body/eval_jaxpr/dot_general | solution.py:52
  200.2 4.7 %fusion.99 = (f32[512]{0:T(512)S(1)}, f32[512]{0:T(512)S(1)}, f32[512,2048]{1,0:T(8,128)S(1)}) fusion(f32[512,2048]{1,0:T(8,128)} %get-tuple-element.270, f32[512]{0:T(512)S(1)} %get-tuple-element.271, s32[512]{0:T(512)S(1)} %dynamic_slice.43, s32[2048]{0:T(1024)S(1)} %get-tuple-element.303, s32[2048]{0:T(1024)S(1)} %get-tuple-element.302, ...), kind=kOutput, calls=%fused_computation.35.clone.1 | convolution fusion | flops 278920192 | bytes 9070600 | tf_op jit(solution)/shard_map/while/body/eval_jaxpr/dot_general | solution.py:52
  212.1 14.0 %copy.50 = bf16[2,2048,1,256]{3,0,2,1:T(2,128)(2,1)} copy(bf16[2,2048,1,256]{3,1,0,2:T(8,128)(2,1)S(1)} %maximum_bitcast_fusion.2) | data formatting | bytes 4194304 | tf_op jit(solution)/shard_map/reshape | solution.py:108
  231.8 28.2 %all-to-all-done.2 = bf16[2,2048,1,256]{3,0,2,1:T(2,128)(2,1)S(1)} async-done(((bf16[2,2048,1,256]{3,0,2,1:T(2,128)(2,1)}), bf16[2,2048,1,256]{3,0,2,1:T(2,128)(2,1)S(1)}, u32[]{:S(2)}, u32[]{:S(2)}) %all-to-all-start.2) | async-done | bytes 2097184 | tf_op jit(solution)/shard_map/all_to_all | solution.py:109
  260.7 26.8 %collective-permute-done = bf16[2,128,16,256]{3,1,2,0:T(8,128)(2,1)} collective-permute-done((bf16[2,128,16,256]{3,1,2,0:T(8,128)(2,1)S(1)}, bf16[2,128,16,256]{3,1,2,0:T(8,128)(2,1)}, u32[]{:S(2)}, u32[]{:S(2)}) %collective-permute-start) | collective-permute-done | bytes 2097184 | tf_op jit(solution)/shard_map/ppermute | solution.py:18
  (120 shorter events, 81.7 us)
Async XLA Ops:
  5.7 39.8 %all-to-all-start = ((bf16[2,128,16,256]{3,1,0,2:T(8,128)(2,1)}), bf16[2,128,16,256]{3,1,0,2:T(8,128)(2,1)S(1)}, u32[]{:S(2)}, u32[]{:S(2)}) async-start(bf16[2,128,16,256]{3,1,0,2:T(8,128)(2,1)} %copy.46), calls=%async_computation | async-start | bytes 4194304 | tf_op jit(solution)/shard_map/all_to_all | solution.py:96
  15.2 36.3 %copy-start.1 = (s32[1,2,4]{2,1,0:T(2,128)S(1)}, s32[1,2,4]{2,1,0:T(2,128)}, u32[]{:S(2)}) copy-start(s32[1,2,4]{2,1,0:T(2,128)} %param.10) | copy-start | bytes 100
  47.1 34.4 %all-to-all-start.1 = ((bf16[2,128,16,256]{3,1,0,2:T(8,128)(2,1)}), bf16[2,128,16,256]{3,1,0,2:T(8,128)(2,1)}, u32[]{:S(2)}, u32[]{:S(2)}) async-start(bf16[2,128,16,256]{3,1,0,2:T(8,128)(2,1)} %bitcast.62), calls=%async_computation.1 | async-start | bytes 4194304 | tf_op jit(solution)/shard_map/all_to_all | solution.py:97
  89.6 4.6 %copy-start.2 = (f32[512,2048]{1,0:T(8,128)S(1)}, f32[512,2048]{1,0:T(8,128)}, u32[]{:S(2)}) copy-start(f32[512,2048]{1,0:T(8,128)} %get-tuple-element.258) | copy-start | bytes 12582916 | tf_op jit(solution)/shard_map/while
  104.4 4.6 %copy-start.2 = (f32[512,2048]{1,0:T(8,128)S(1)}, f32[512,2048]{1,0:T(8,128)}, u32[]{:S(2)}) copy-start(f32[512,2048]{1,0:T(8,128)} %get-tuple-element.258) | copy-start | bytes 12582916 | tf_op jit(solution)/shard_map/while
  119.2 4.6 %copy-start.2 = (f32[512,2048]{1,0:T(8,128)S(1)}, f32[512,2048]{1,0:T(8,128)}, u32[]{:S(2)}) copy-start(f32[512,2048]{1,0:T(8,128)} %get-tuple-element.258) | copy-start | bytes 12582916 | tf_op jit(solution)/shard_map/while
  133.9 4.6 %copy-start.2 = (f32[512,2048]{1,0:T(8,128)S(1)}, f32[512,2048]{1,0:T(8,128)}, u32[]{:S(2)}) copy-start(f32[512,2048]{1,0:T(8,128)} %get-tuple-element.258) | copy-start | bytes 12582916 | tf_op jit(solution)/shard_map/while
  149.1 4.7 %copy-start.3 = (f32[512,2048]{1,0:T(8,128)S(1)}, f32[512,2048]{1,0:T(8,128)}, u32[]{:S(2)}) copy-start(f32[512,2048]{1,0:T(8,128)} %get-tuple-element.270) | copy-start | bytes 12582916 | tf_op jit(solution)/shard_map/while
  166.1 4.7 %copy-start.3 = (f32[512,2048]{1,0:T(8,128)S(1)}, f32[512,2048]{1,0:T(8,128)}, u32[]{:S(2)}) copy-start(f32[512,2048]{1,0:T(8,128)} %get-tuple-element.270) | copy-start | bytes 12582916 | tf_op jit(solution)/shard_map/while
  183.2 4.7 %copy-start.3 = (f32[512,2048]{1,0:T(8,128)S(1)}, f32[512,2048]{1,0:T(8,128)}, u32[]{:S(2)}) copy-start(f32[512,2048]{1,0:T(8,128)} %get-tuple-element.270) | copy-start | bytes 12582916 | tf_op jit(solution)/shard_map/while
  200.2 4.7 %copy-start.3 = (f32[512,2048]{1,0:T(8,128)S(1)}, f32[512,2048]{1,0:T(8,128)}, u32[]{:S(2)}) copy-start(f32[512,2048]{1,0:T(8,128)} %get-tuple-element.270) | copy-start | bytes 12582916 | tf_op jit(solution)/shard_map/while
  212.0 17.7 %copy-start = (s32[1,2]{1,0:T(1,128)S(1)}, s32[1,2]{1,0:T(1,128)}, u32[]{:S(2)}) copy-start(s32[1,2]{1,0:T(1,128)} %param.11) | copy-start | bytes 28
  226.1 33.9 %all-to-all-start.2 = ((bf16[2,2048,1,256]{3,0,2,1:T(2,128)(2,1)}), bf16[2,2048,1,256]{3,0,2,1:T(2,128)(2,1)S(1)}, u32[]{:S(2)}, u32[]{:S(2)}) async-start(bf16[2,2048,1,256]{3,0,2,1:T(2,128)(2,1)} %copy.50), calls=%async_computation.2 | async-start | bytes 4194304 | tf_op jit(solution)/shard_map/all_to_all | solution.py:109
  260.7 26.8 %collective-permute-start = (bf16[2,128,16,256]{3,1,2,0:T(8,128)(2,1)S(1)}, bf16[2,128,16,256]{3,1,2,0:T(8,128)(2,1)}, u32[]{:S(2)}, u32[]{:S(2)}) collective-permute-start(bf16[2,128,16,256]{3,1,2,0:T(8,128)(2,1)S(1)} %pad_maximum_fusion), channel_id=1, source_target_pairs={{112,0},{0,16},{16,32},{32,48},{48,64},{64,80},{80,96},{96,112},{1... | collective-permute-start | bytes 6291464 | tf_op jit(solution)/shard_map/ppermute | solution.py:18
where the time goes:
time: 294 us; the launch traced here: 293 us
  waiting for transfers between devices  113 us (38%)
  matrix products  99.9 us (34%)
  local copies, waits for them, and re-layouts  41.4 us (14%)
  starting transfers between devices  16.2 us (6%)
  other arithmetic  15.1 us (5%)
  loops' own time  6.04 us (2%)
    dot_general x16, matrix products, one_block(): lax.dot_general(query_cols, key_cols, (((1,), (1,)), ((), ())), preferred...  68.2 us
    dot_general x16, matrix products, one_block(): jnp.dot(weights.astype(jnp.bfloat16), value_cols, preferred_element_type=...  31.6 us
    all_to_all x1, waiting for transfers between devices, local(): lax.all_to_all(query_split, 'seq', split_axis=2, concat_axis=1, tiled=True)  30.3 us
    all_to_all x1, waiting for transfers between devices, local(): lax.all_to_all(shortened(contexts), 'seq', split_axis=1, concat_axis=2, t...  28.2 us
    all_to_all x1, waiting for transfers between devices, local(): lax.all_to_all(wide, 'seq', split_axis=2, concat_axis=1, tiled=True)  27.9 us
    ppermute x1, waiting for transfers between devices, passed_along(): return lax.ppermute(block, axis, route)  26.8 us
    reshape x1, local copies, waits for them, and re-layouts, local(): contexts = contexts.reshape(micro, all_rows, 1, per_device * HD)  14 us
    reduce_sum x8, other arithmetic, one_block(): totals = jnp.sum(weights, axis=1, keepdims=True)  13.8 us
  transfers between devices with their start and end apart: 4, of which 4 were waited for; matrix products, arithmetic and copies ran while one was open for 1% of the time, Pallas kernels for 0%

commit v1 on v0

--- a/solution.py
+++ b/solution.py
@@ -6,6 +6,18 @@
 HD = 128
 QH = 32
 KVH = 8
+
+
+def sent_to_each(x, axis, split, join):
+    ways, here = (lax.axis_size(axis), lax.axis_index(axis))
+    width = x.shape[split] // ways
+    turned = jnp.roll(x, -here * width, axis=split)
+    got = [lax.slice_in_dim(turned, 0, width, axis=split)]
+    for far in range(1, ways):
+        sent = lax.slice_in_dim(turned, far * width, (far + 1) * width, axis=split)
+        got.append(lax.ppermute(sent, axis, [(d, (d + far) % ways) for d in range(ways)]))
+    line = jnp.concatenate(got[::-1], axis=join)
+    return jnp.roll(line, (here + 1) * got[0].shape[join], axis=join)
 
 
 def shortened(value):
@@ -93,7 +105,7 @@
     query_split = queries.reshape(micro, tok_rows, n_seq, per_device * HD)
     wide = jnp.repeat(keys_values.reshape(micro, tok_rows, KVH, 2 * HD), repeat_count, axis=2)
     head_queries, head_pairs = (
-        lax.all_to_all(query_split, "seq", split_axis=2, concat_axis=1, tiled=True),
+        sent_to_each(query_split, "seq", 2, 1),
         lax.all_to_all(wide, "seq", split_axis=2, concat_axis=1, tiled=True),
     )
     head_queries = head_queries.reshape(micro, all_rows, per_device * HD)

time: 294 us -> 294 us (level)
  starting transfers between devices: 16.2 us -> 45.5 us
  waiting for transfers between devices: 113 us -> 83.8 us
  matrix products: 99.9 us -> 94.3 us
    ppermute x0 -> x15, starting transfers between devices: none -> 35.3 us  [sent_to_each(): lax.ppermute(sent, axis, [(d, (d + far) % ways) for d in range(ways)])]
    ppermute x0 -> x15, waiting for transfers between devices: none -> 31.2 us  [sent_to_each(): lax.ppermute(sent, axis, [(d, (d + far) % ways) for d in range(ways)])]
    all_to_all x1 -> x0, waiting for transfers between devices: 30.3 us -> none  [local(): lax.all_to_all(query_split, 'seq', split_axis=2, concat_axis=1, tiled=True)]
    all_to_all x1, waiting for transfers between devices: 27.9 us -> 0.01 us  [local(): lax.all_to_all(wide, 'seq', split_axis=2, concat_axis=1, tiled=True)]
    dot_general x16, matrix products: 31.6 us -> 23.5 us  [one_block(): jnp.dot(weights.astype(jnp.bfloat16), value_cols, preferred_element_type=...]
    all_to_all x1 -> x0, starting transfers between devices: 7.99 us -> none  [local(): lax.all_to_all(query_split, 'seq', split_axis=2, concat_axis=1, tiled=True)]
    unnamed x5 -> x44, local copies, waits for them, and re-layouts: 3.14 us -> 8.87 us
  transfers between devices with their start and end apart: 4 -> 18, of which waited for: 4 -> 7; matrix products, arithmetic and copies ran while one was open for 1% -> 3% of each run, Pallas kernels for 0% -> 0%
where the time goes in v1:
time: 294 us; the launch traced here: 293 us
  matrix products  94.3 us (32%)
  waiting for transfers between devices  83.8 us (29%)
  starting transfers between devices  45.5 us (15%)
  local copies, waits for them, and re-layouts  44.2 us (15%)
  other arithmetic  17.6 us (6%)
  loops' own time  5.72 us (2%)
    dot_general x16, matrix products, one_block(): lax.dot_general(query_cols, key_cols, (((1,), (1,)), ((), ())), preferred...  70.8 us
    ppermute x15, starting transfers between devices, sent_to_each(): lax.ppermute(sent, axis, [(d, (d + far) % ways) for d in range(ways)])  35.3 us
    ppermute x15, waiting for transfers between devices, sent_to_each(): lax.ppermute(sent, axis, [(d, (d + far) % ways) for d in range(ways)])  31.2 us
    ppermute x1, waiting for transfers between devices, passed_along(): return lax.ppermute(block, axis, route)  26.8 us
    all_to_all x1, waiting for transfers between devices, local(): lax.all_to_all(shortened(contexts), 'seq', split_axis=1, concat_axis=2, t...  25.8 us
    dot_general x16, matrix products, one_block(): jnp.dot(weights.astype(jnp.bfloat16), value_cols, preferred_element_type=...  23.5 us
    reshape x1, local copies, waits for them, and re-layouts, local(): contexts = contexts.reshape(micro, all_rows, 1, per_device * HD)  14 us
    reduce_sum x8, other arithmetic, one_block(): totals = jnp.sum(weights, axis=1, keepdims=True)  13.8 us
  transfers between devices with their start and end apart: 18, of which 7 were waited for; matrix products, arithmetic and copies ran while one was open for 3% of the time, Pallas kernels for 0%

profile of v1, /device:TPU:0, one launch (start us, length us, event | category | flops | bytes accessed | tf_op | source)
XLA Modules:
  0.0 292.9 jit_solution(15124902686634250611)
XLA Ops:
  7.8 6.4 %collective-permute-start = (bf16[2,128,1,256]{1,3,2,0:T(8,128)(2,1)}, bf16[2,128,1,256]{1,3,2,0:T(8,128)(2,1)S(1)}, u32[]{:S(2)}, u32[]{:S(2)}) collective-permute-start(bf16[2,128,1,256]{1,3,2,0:T(8,128)(2,1)} %get-tuple-element.235), channel_id=1, source_target_pairs={{0,15},{1,0},{2,1},{3,2},{4,3},{5,4},{6,5},{7,6},{8,7},{9,8},{10,9... | collective-permute-start | bytes 393224 | tf_op jit(solution)/shard_map/ppermute | solution.py:18
  19.5 6.5 %all-to-all-start = ((bf16[2,128,16,256]{3,1,0,2:T(8,128)(2,1)}), bf16[2,128,16,256]{3,1,0,2:T(8,128)(2,1)}, u32[]{:S(2)}, u32[]{:S(2)}) async-start(bf16[2,128,16,256]{3,1,0,2:T(8,128)(2,1)} %bitcast.60), calls=%async_computation | async-start | bytes 4194304 | tf_op jit(solution)/shard_map/all_to_all | solution.py:109
  26.6 5.9 %collective-permute-start.5 = (bf16[2,128,1,256]{1,3,2,0:T(8,128)(2,1)S(1)}, bf16[2,128,1,256]{1,3,2,0:T(8,128)(2,1)S(1)}, u32[]{:S(2)}, u32[]{:S(2)}) collective-permute-start(bf16[2,128,1,256]{1,3,2,0:T(8,128)(2,1)S(1)} %copy-done.5), channel_id=1, source_target_pairs={{0,10},{1,11},{2,12},{3,13},{4,14},{5,15},{6,0},{7,1},{8,2},{9,3},... | collective-permute-start | bytes 393224 | tf_op jit(solution)/shard_map/ppermute | solution.py:18
  40.6 18.8 %collective-permute-done.5 = bf16[2,128,1,256]{1,3,2,0:T(8,128)(2,1)S(1)} collective-permute-done((bf16[2,128,1,256]{1,3,2,0:T(8,128)(2,1)S(1)}, bf16[2,128,1,256]{1,3,2,0:T(8,128)(2,1)S(1)}, u32[]{:S(2)}, u32[]{:S(2)}) %collective-permute-start.5) | collective-permute-done | bytes 131104 | tf_op jit(solution)/shard_map/ppermute | solution.py:18
  63.6 11.9 %collective-permute-start.12 = (bf16[2,128,1,256]{1,3,2,0:T(8,128)(2,1)}, bf16[2,128,1,256]{1,3,2,0:T(8,128)(2,1)S(1)}, u32[]{:S(2)}, u32[]{:S(2)}) collective-permute-start(bf16[2,128,1,256]{1,3,2,0:T(8,128)(2,1)} %get-tuple-element.223), channel_id=1, source_target_pairs={{0,3},{1,4},{2,5},{3,6},{4,7},{5,8},{6,9},{7,10},{8,11},{9,12},{10... | collective-permute-start | bytes 393224 | tf_op jit(solution)/shard_map/ppermute | solution.py:18
  79.8 4.7 %collective-permute-done.13 = bf16[2,128,1,256]{1,3,2,0:T(8,128)(2,1)S(1)} collective-permute-done((bf16[2,128,1,256]{1,3,2,0:T(8,128)(2,1)}, bf16[2,128,1,256]{1,3,2,0:T(8,128)(2,1)S(1)}, u32[]{:S(2)}, u32[]{:S(2)}) %collective-permute-start.13) | collective-permute-done | bytes 131104 | tf_op jit(solution)/shard_map/ppermute | solution.py:18
  92.8 59.5 %while.22 = (s32[]{:T(128)}, bf16[4,512,256]{2,1,0:T(8,128)(2,1)S(1)}, s32[4]{0:T(128)S(1)}, s32[2048]{0:T(1024)S(1)}, s32[2048]{0:T(1024)S(1)}, /*index=5*/bf16...) while((s32[]{:T(128)}, ...), condition=%wide.region_7.8_spmd.clone, body=%wide.region_2.7_spmd.clone.sunk | while | flops 1113323520 | bytes 50462988 | solution.py:84
  98.4 4.4 %fusion.92 = (f32[512]{0:T(512)S(1)}, f32[512]{0:T(512)S(1)}, f32[512,2048]{1,0:T(8,128)S(1)}) fusion(f32[512,2048]{1,0:T(8,128)} %get-tuple-element.329, f32[512]{0:T(512)S(1)} %get-tuple-element.330, s32[512]{0:T(512)S(1)} %dynamic_slice.58, s32[2048]{0:T(1024)S(1)} %get-tuple-element.410, s32[2048]{0:T(1024)S(1)} %get-tuple-element.409, ...), kind=kOutput, calls=%fused_computation.5.clone.1 | convolution fusion | flops 278920192 | bytes 9070600 | tf_op jit(solution)/shard_map/while/body/eval_jaxpr/dot_general | solution.py:64
  109.0 4.2 %select_reduce_fusion.6 = (f32[512]{0:T(512)S(1)}, f32[512,2048]{1,0:T(8,128)}) fusion(s32[512]{0:T(512)S(1)} %dynamic_slice.58, s32[2048]{0:T(1024)S(1)} %get-tuple-element.410, s32[2048]{0:T(1024)S(1)} %get-tuple-element.409, s32[512]{0:T(512)S(1)} %dynamic_slice.59, bf16[2048,256]{1,0:T(8,128)(2,1)} %get-tuple-element.412, ...), kind=kOutput, calls=%fused_computation.3.clone.1 | convolution fusion | flops 274726400 | bytes 4872196 | tf_op jit(solution)/shard_map/while/body/eval_jaxpr/dot_general | solution.py:64
  113.2 4.4 %fusion.92 = (f32[512]{0:T(512)S(1)}, f32[512]{0:T(512)S(1)}, f32[512,2048]{1,0:T(8,128)S(1)}) fusion(f32[512,2048]{1,0:T(8,128)} %get-tuple-element.329, f32[512]{0:T(512)S(1)} %get-tuple-element.330, s32[512]{0:T(512)S(1)} %dynamic_slice.58, s32[2048]{0:T(1024)S(1)} %get-tuple-element.410, s32[2048]{0:T(1024)S(1)} %get-tuple-element.409, ...), kind=kOutput, calls=%fused_computation.5.clone.1 | convolution fusion | flops 278920192 | bytes 9070600 | tf_op jit(solution)/shard_map/while/body/eval_jaxpr/dot_general | solution.py:64
  128.1 4.4 %fusion.92 = (f32[512]{0:T(512)S(1)}, f32[512]{0:T(512)S(1)}, f32[512,2048]{1,0:T(8,128)S(1)}) fusion(f32[512,2048]{1,0:T(8,128)} %get-tuple-element.329, f32[512]{0:T(512)S(1)} %get-tuple-element.330, s32[512]{0:T(512)S(1)} %dynamic_slice.58, s32[2048]{0:T(1024)S(1)} %get-tuple-element.410, s32[2048]{0:T(1024)S(1)} %get-tuple-element.409, ...), kind=kOutput, calls=%fused_computation.5.clone.1 | convolution fusion | flops 278920192 | bytes 9070600 | tf_op jit(solution)/shard_map/while/body/eval_jaxpr/dot_general | solution.py:64
  143.0 4.4 %fusion.92 = (f32[512]{0:T(512)S(1)}, f32[512]{0:T(512)S(1)}, f32[512,2048]{1,0:T(8,128)S(1)}) fusion(f32[512,2048]{1,0:T(8,128)} %get-tuple-element.329, f32[512]{0:T(512)S(1)} %get-tuple-element.330, s32[512]{0:T(512)S(1)} %dynamic_slice.58, s32[2048]{0:T(1024)S(1)} %get-tuple-element.410, s32[2048]{0:T(1024)S(1)} %get-tuple-element.409, ...), kind=kOutput, calls=%fused_computation.5.clone.1 | convolution fusion | flops 278920192 | bytes 9070600 | tf_op jit(solution)/shard_map/while/body/eval_jaxpr/dot_general | solution.py:64
  152.4 61.7 %while.23 = (s32[]{:T(128)}, bf16[4,512,256]{2,1,0:T(8,128)(2,1)S(1)}, s32[4]{0:T(128)S(1)}, s32[2048]{0:T(1024)S(1)}, s32[2048]{0:T(1024)S(1)}, /*index=5*/bf16...) while((s32[]{:T(128)}, ...), condition=%wide.region_15.16_spmd.clone, body=%wide.region_10.15_spmd.clone.sunk | while | flops 1113323520 | bytes 50462988 | solution.py:84
  154.0 4.3 %select_reduce_fusion.7 = (f32[512]{0:T(512)S(1)}, f32[512,2048]{1,0:T(8,128)}) fusion(s32[512]{0:T(512)S(1)} %dynamic_slice.61, s32[2048]{0:T(1024)S(1)} %get-tuple-element.374, s32[2048]{0:T(1024)S(1)} %get-tuple-element.373, s32[512]{0:T(512)S(1)} %dynamic_slice.62, bf16[2048,256]{1,0:T(8,128)(2,1)} %get-tuple-element.376, ...), kind=kOutput, calls=%fused_computation.33.clone.1 | convolution fusion | flops 274726400 | bytes 4872196 | tf_op jit(solution)/shard_map/while/body/eval_jaxpr/dot_general | solution.py:64
  158.3 4.8 %fusion.100 = (f32[512]{0:T(512)S(1)}, f32[512]{0:T(512)S(1)}, f32[512,2048]{1,0:T(8,128)S(1)}) fusion(f32[512,2048]{1,0:T(8,128)} %get-tuple-element.341, f32[512]{0:T(512)S(1)} %get-tuple-element.342, s32[512]{0:T(512)S(1)} %dynamic_slice.61, s32[2048]{0:T(1024)S(1)} %get-tuple-element.374, s32[2048]{0:T(1024)S(1)} %get-tuple-element.373, ...), kind=kOutput, calls=%fused_computation.35.clone.1 | convolution fusion | flops 278920192 | bytes 9070600 | tf_op jit(solution)/shard_map/while/body/eval_jaxpr/dot_general | solution.py:64
  169.4 4.3 %select_reduce_fusion.7 = (f32[512]{0:T(512)S(1)}, f32[512,2048]{1,0:T(8,128)}) fusion(s32[512]{0:T(512)S(1)} %dynamic_slice.61, s32[2048]{0:T(1024)S(1)} %get-tuple-element.374, s32[2048]{0:T(1024)S(1)} %get-tuple-element.373, s32[512]{0:T(512)S(1)} %dynamic_slice.62, bf16[2048,256]{1,0:T(8,128)(2,1)} %get-tuple-element.376, ...), kind=kOutput, calls=%fused_computation.33.clone.1 | convolution fusion | flops 274726400 | bytes 4872196 | tf_op jit(solution)/shard_map/while/body/eval_jaxpr/dot_general | solution.py:64
  173.7 4.8 %fusion.100 = (f32[512]{0:T(512)S(1)}, f32[512]{0:T(512)S(1)}, f32[512,2048]{1,0:T(8,128)S(1)}) fusion(f32[512,2048]{1,0:T(8,128)} %get-tuple-element.341, f32[512]{0:T(512)S(1)} %get-tuple-element.342, s32[512]{0:T(512)S(1)} %dynamic_slice.61, s32[2048]{0:T(1024)S(1)} %get-tuple-element.374, s32[2048]{0:T(1024)S(1)} %get-tuple-element.373, ...), kind=kOutput, calls=%fused_computation.35.clone.1 | convolution fusion | flops 278920192 | bytes 9070600 | tf_op jit(solution)/shard_map/while/body/eval_jaxpr/dot_general | solution.py:64
  184.8 4.3 %select_reduce_fusion.7 = (f32[512]{0:T(512)S(1)}, f32[512,2048]{1,0:T(8,128)}) fusion(s32[512]{0:T(512)S(1)} %dynamic_slice.61, s32[2048]{0:T(1024)S(1)} %get-tuple-element.374, s32[2048]{0:T(1024)S(1)} %get-tuple-element.373, s32[512]{0:T(512)S(1)} %dynamic_slice.62, bf16[2048,256]{1,0:T(8,128)(2,1)} %get-tuple-element.376, ...), kind=kOutput, calls=%fused_computation.33.clone.1 | convolution fusion | flops 274726400 | bytes 4872196 | tf_op jit(solution)/shard_map/while/body/eval_jaxpr/dot_general | solution.py:64
  189.1 4.8 %fusion.100 = (f32[512]{0:T(512)S(1)}, f32[512]{0:T(512)S(1)}, f32[512,2048]{1,0:T(8,128)S(1)}) fusion(f32[512,2048]{1,0:T(8,128)} %get-tuple-element.341, f32[512]{0:T(512)S(1)} %get-tuple-element.342, s32[512]{0:T(512)S(1)} %dynamic_slice.61, s32[2048]{0:T(1024)S(1)} %get-tuple-element.374, s32[2048]{0:T(1024)S(1)} %get-tuple-element.373, ...), kind=kOutput, calls=%fused_computation.35.clone.1 | convolution fusion | flops 278920192 | bytes 9070600 | tf_op jit(solution)/shard_map/while/body/eval_jaxpr/dot_general | solution.py:64
  200.1 4.3 %select_reduce_fusion.7 = (f32[512]{0:T(512)S(1)}, f32[512,2048]{1,0:T(8,128)}) fusion(s32[512]{0:T(512)S(1)} %dynamic_slice.61, s32[2048]{0:T(1024)S(1)} %get-tuple-element.374, s32[2048]{0:T(1024)S(1)} %get-tuple-element.373, s32[512]{0:T(512)S(1)} %dynamic_slice.62, bf16[2048,256]{1,0:T(8,128)(2,1)} %get-tuple-element.376, ...), kind=kOutput, calls=%fused_computation.33.clone.1 | convolution fusion | flops 274726400 | bytes 4872196 | tf_op jit(solution)/shard_map/while/body/eval_jaxpr/dot_general | solution.py:64
  204.4 4.8 %fusion.100 = (f32[512]{0:T(512)S(1)}, f32[512]{0:T(512)S(1)}, f32[512,2048]{1,0:T(8,128)S(1)}) fusion(f32[512,2048]{1,0:T(8,128)} %get-tuple-element.341, f32[512]{0:T(512)S(1)} %get-tuple-element.342, s32[512]{0:T(512)S(1)} %dynamic_slice.61, s32[2048]{0:T(1024)S(1)} %get-tuple-element.374, s32[2048]{0:T(1024)S(1)} %get-tuple-element.373, ...), kind=kOutput, calls=%fused_computation.35.clone.1 | convolution fusion | flops 278920192 | bytes 9070600 | tf_op jit(solution)/shard_map/while/body/eval_jaxpr/dot_general | solution.py:64
  214.3 14.0 %copy.45 = bf16[2,2048,1,256]{3,0,2,1:T(2,128)(2,1)} copy(bf16[2,2048,1,256]{3,1,0,2:T(8,128)(2,1)S(1)} %maximum_bitcast_fusion.2) | data formatting | bytes 4194304 | tf_op jit(solution)/shard_map/reshape | solution.py:120
  233.8 25.8 %all-to-all-done.1 = bf16[2,2048,1,256]{3,0,2,1:T(2,128)(2,1)S(1)} async-done(((bf16[2,2048,1,256]{3,0,2,1:T(2,128)(2,1)}), bf16[2,2048,1,256]{3,0,2,1:T(2,128)(2,1)S(1)}, u32[]{:S(2)}, u32[]{:S(2)}) %all-to-all-start.1) | async-done | bytes 2097184 | tf_op jit(solution)/shard_map/all_to_all | solution.py:121
  260.3 26.8 %collective-permute-done.15 = bf16[2,128,16,256]{3,1,2,0:T(8,128)(2,1)} collective-permute-done((bf16[2,128,16,256]{3,1,2,0:T(8,128)(2,1)S(1)}, bf16[2,128,16,256]{3,1,2,0:T(8,128)(2,1)}, u32[]{:S(2)}, u32[]{:S(2)}) %collective-permute-start.15) | collective-permute-done | bytes 2097184 | tf_op jit(solution)/shard_map/ppermute | solution.py:30
  (205 shorter events, 106.5 us)
Async XLA Ops:
  4.1 13.6 %copy-start = (bf16[1,2,128,8,256]{4,3,2,1,0:T(8,128)(2,1)S(1)}, bf16[1,2,128,8,256]{4,3,2,1,0:T(8,128)(2,1)}, u32[]{:S(2)}) copy-start(bf16[1,2,128,8,256]{4,3,2,1,0:T(8,128)(2,1)} %param.9) | copy-start | bytes 3145732
  7.8 18.8 %collective-permute-start = (bf16[2,128,1,256]{1,3,2,0:T(8,128)(2,1)}, bf16[2,128,1,256]{1,3,2,0:T(8,128)(2,1)S(1)}, u32[]{:S(2)}, u32[]{:S(2)}) collective-permute-start(bf16[2,128,1,256]{1,3,2,0:T(8,128)(2,1)} %get-tuple-element.235), channel_id=1, source_target_pairs={{0,15},{1,0},{2,1},{3,2},{4,3},{5,4},{6,5},{7,6},{8,7},{9,8},{10,9... | collective-permute-start | bytes 393224 | tf_op jit(solution)/shard_map/ppermute | solution.py:18
  14.2 18.3 %collective-permute-start.1 = (bf16[2,128,1,256]{1,3,2,0:T(8,128)(2,1)}, bf16[2,128,1,256]{1,3,2,0:T(8,128)(2,1)S(1)}, u32[]{:S(2)}, u32[]{:S(2)}) collective-permute-start(bf16[2,128,1,256]{1,3,2,0:T(8,128)(2,1)} %get-tuple-element.234), channel_id=1, source_target_pairs={{0,14},{1,15},{2,0},{3,1},{4,2},{5,3},{6,4},{7,5},{8,6},{9,7},{10,... | collective-permute-start | bytes 393224 | tf_op jit(solution)/shard_map/ppermute | solution.py:18
  14.9 18.2 %collective-permute-start.2 = (bf16[2,128,1,256]{1,3,2,0:T(8,128)(2,1)}, bf16[2,128,1,256]{1,3,2,0:T(8,128)(2,1)S(1)}, u32[]{:S(2)}, u32[]{:S(2)}) collective-permute-start(bf16[2,128,1,256]{1,3,2,0:T(8,128)(2,1)} %get-tuple-element.233), channel_id=1, source_target_pairs={{0,13},{1,14},{2,15},{3,0},{4,1},{5,2},{6,3},{7,4},{8,5},{9,6},{10... | collective-permute-start | bytes 393224 | tf_op jit(solution)/shard_map/ppermute | solution.py:18
  15.6 20.6 %collective-permute-start.3 = (bf16[2,128,1,256]{1,3,2,0:T(8,128)(2,1)}, bf16[2,128,1,256]{1,3,2,0:T(8,128)(2,1)}, u32[]{:S(2)}, u32[]{:S(2)}) collective-permute-start(bf16[2,128,1,256]{1,3,2,0:T(8,128)(2,1)} %get-tuple-element.232), channel_id=1, source_target_pairs={{0,12},{1,13},{2,14},{3,15},{4,0},{5,1},{6,2},{7,3},{8,4},{9,5},{1... | collective-permute-start | bytes 393224 | tf_op jit(solution)/shard_map/ppermute | solution.py:18
  15.7 22.2 %collective-permute-start.4 = (bf16[2,128,1,256]{1,3,2,0:T(8,128)(2,1)}, bf16[2,128,1,256]{1,3,2,0:T(8,128)(2,1)}, u32[]{:S(2)}, u32[]{:S(2)}) collective-permute-start(bf16[2,128,1,256]{1,3,2,0:T(8,128)(2,1)} %get-tuple-element.231), channel_id=1, source_target_pairs={{0,11},{1,12},{2,13},{3,14},{4,15},{5,0},{6,1},{7,2},{8,3},{9,4},{... | collective-permute-start | bytes 393224 | tf_op jit(solution)/shard_map/ppermute | solution.py:18
  17.9 8.1 %copy-start.7 = (s32[1,2,4]{2,1,0:T(2,128)S(1)}, s32[1,2,4]{2,1,0:T(2,128)}, u32[]{:S(2)}) copy-start(s32[1,2,4]{2,1,0:T(2,128)} %param.10) | copy-start | bytes 100
  17.9 8.7 %copy-start.5 = (bf16[2,128,1,256]{1,3,2,0:T(8,128)(2,1)S(1)}, bf16[2,128,1,256]{1,3,2,0:T(8,128)(2,1)}, u32[]{:S(2)}) copy-start(bf16[2,128,1,256]{1,3,2,0:T(8,128)(2,1)} %get-tuple-element.230) | copy-start | bytes 393220
  17.9 14.6 %copy-start.4 = (bf16[2,128,1,256]{1,3,2,0:T(8,128)(2,1)S(1)}, bf16[2,128,1,256]{1,3,2,0:T(8,128)(2,1)}, u32[]{:S(2)}) copy-start(bf16[2,128,1,256]{1,3,2,0:T(8,128)(2,1)} %get-tuple-element.229) | copy-start | bytes 393220
  17.9 15.3 %copy-start.3 = (bf16[2,128,1,256]{1,3,2,0:T(8,128)(2,1)S(1)}, bf16[2,128,1,256]{1,3,2,0:T(8,128)(2,1)}, u32[]{:S(2)}) copy-start(bf16[2,128,1,256]{1,3,2,0:T(8,128)(2,1)} %get-tuple-element.228) | copy-start | bytes 393220
  19.5 70.2 %all-to-all-start = ((bf16[2,128,16,256]{3,1,0,2:T(8,128)(2,1)}), bf16[2,128,16,256]{3,1,0,2:T(8,128)(2,1)}, u32[]{:S(2)}, u32[]{:S(2)}) async-start(bf16[2,128,16,256]{3,1,0,2:T(8,128)(2,1)} %bitcast.60), calls=%async_computation | async-start | bytes 4194304 | tf_op jit(solution)/shard_map/all_to_all | solution.py:109
  26.6 32.8 %collective-permute-start.5 = (bf16[2,128,1,256]{1,3,2,0:T(8,128)(2,1)S(1)}, bf16[2,128,1,256]{1,3,2,0:T(8,128)(2,1)S(1)}, u32[]{:S(2)}, u32[]{:S(2)}) collective-permute-start(bf16[2,128,1,256]{1,3,2,0:T(8,128)(2,1)S(1)} %copy-done.5), channel_id=1, source_target_pairs={{0,10},{1,11},{2,12},{3,13},{4,14},{5,15},{6,0},{7,1},{8,2},{9,3},... | collective-permute-start | bytes 393224 | tf_op jit(solution)/shard_map/ppermute | solution.py:18
  32.5 31.0 %collective-permute-start.6 = (bf16[2,128,1,256]{1,3,2,0:T(8,128)(2,1)S(1)}, bf16[2,128,1,256]{1,3,2,0:T(8,128)(2,1)S(1)}, u32[]{:S(2)}, u32[]{:S(2)}) collective-permute-start(bf16[2,128,1,256]{1,3,2,0:T(8,128)(2,1)S(1)} %copy-done.4), channel_id=1, source_target_pairs={{0,9},{1,10},{2,11},{3,12},{4,13},{5,14},{6,15},{7,0},{8,1},{9,2},... | collective-permute-start | bytes 393224 | tf_op jit(solution)/shard_map/ppermute | solution.py:18
  33.2 30.4 %collective-permute-start.7 = (bf16[2,128,1,256]{1,3,2,0:T(8,128)(2,1)S(1)}, bf16[2,128,1,256]{1,3,2,0:T(8,128)(2,1)S(1)}, u32[]{:S(2)}, u32[]{:S(2)}) collective-permute-start(bf16[2,128,1,256]{1,3,2,0:T(8,128)(2,1)S(1)} %copy-done.3), channel_id=1, source_target_pairs={{0,8},{1,9},{2,10},{3,11},{4,12},{5,13},{6,14},{7,15},{8,0},{9,1},... | collective-permute-start | bytes 393224 | tf_op jit(solution)/shard_map/ppermute | solution.py:18
  36.3 39.2 %collective-permute-start.8 = (bf16[2,128,1,256]{1,3,2,0:T(8,128)(2,1)}, bf16[2,128,1,256]{1,3,2,0:T(8,128)(2,1)S(1)}, u32[]{:S(2)}, u32[]{:S(2)}) collective-permute-start(bf16[2,128,1,256]{1,3,2,0:T(8,128)(2,1)} %get-tuple-element.227), channel_id=1, source_target_pairs={{0,7},{1,8},{2,9},{3,10},{4,11},{5,12},{6,13},{7,14},{8,15},{9,0},... | collective-permute-start | bytes 393224 | tf_op jit(solution)/shard_map/ppermute | solution.py:18
  37.9 37.7 %collective-permute-start.9 = (bf16[2,128,1,256]{1,3,2,0:T(8,128)(2,1)}, bf16[2,128,1,256]{1,3,2,0:T(8,128)(2,1)S(1)}, u32[]{:S(2)}, u32[]{:S(2)}) collective-permute-start(bf16[2,128,1,256]{1,3,2,0:T(8,128)(2,1)} %get-tuple-element.226), channel_id=1, source_target_pairs={{0,6},{1,7},{2,8},{3,9},{4,10},{5,11},{6,12},{7,13},{8,14},{9,15},... | collective-permute-start | bytes 393224 | tf_op jit(solution)/shard_map/ppermute | solution.py:18
  59.4 17.4 %collective-permute-start.10 = (bf16[2,128,1,256]{1,3,2,0:T(8,128)(2,1)}, bf16[2,128,1,256]{1,3,2,0:T(8,128)(2,1)S(1)}, u32[]{:S(2)}, u32[]{:S(2)}) collective-permute-start(bf16[2,128,1,256]{1,3,2,0:T(8,128)(2,1)} %get-tuple-element.225), channel_id=1, source_target_pairs={{0,5},{1,6},{2,7},{3,8},{4,9},{5,10},{6,11},{7,12},{8,13},{9,14},{... | collective-permute-start | bytes 393224 | tf_op jit(solution)/shard_map/ppermute | solution.py:18
  63.5 13.4 %collective-permute-start.11 = (bf16[2,128,1,256]{1,3,2,0:T(8,128)(2,1)}, bf16[2,128,1,256]{1,3,2,0:T(8,128)(2,1)S(1)}, u32[]{:S(2)}, u32[]{:S(2)}) collective-permute-start(bf16[2,128,1,256]{1,3,2,0:T(8,128)(2,1)} %get-tuple-element.224), channel_id=1, source_target_pairs={{0,4},{1,5},{2,6},{3,7},{4,8},{5,9},{6,10},{7,11},{8,12},{9,13},{1... | collective-permute-start | bytes 393224 | tf_op jit(solution)/shard_map/ppermute | solution.py:18
  63.6 16.2 %collective-permute-start.12 = (bf16[2,128,1,256]{1,3,2,0:T(8,128)(2,1)}, bf16[2,128,1,256]{1,3,2,0:T(8,128)(2,1)S(1)}, u32[]{:S(2)}, u32[]{:S(2)}) collective-permute-start(bf16[2,128,1,256]{1,3,2,0:T(8,128)(2,1)} %get-tuple-element.223), channel_id=1, source_target_pairs={{0,3},{1,4},{2,5},{3,6},{4,7},{5,8},{6,9},{7,10},{8,11},{9,12},{10... | collective-permute-start | bytes 393224 | tf_op jit(solution)/shard_map/ppermute | solution.py:18
  75.5 9.0 %collective-permute-start.13 = (bf16[2,128,1,256]{1,3,2,0:T(8,128)(2,1)}, bf16[2,128,1,256]{1,3,2,0:T(8,128)(2,1)S(1)}, u32[]{:S(2)}, u32[]{:S(2)}) collective-permute-start(bf16[2,128,1,256]{1,3,2,0:T(8,128)(2,1)} %get-tuple-element.222), channel_id=1, source_target_pairs={{0,2},{1,3},{2,4},{3,5},{4,6},{5,7},{6,8},{7,9},{8,10},{9,11},{10,... | collective-permute-start | bytes 393224 | tf_op jit(solution)/shard_map/ppermute | solution.py:18
  75.7 10.1 %collective-permute-start.14 = (bf16[2,128,1,256]{1,3,2,0:T(8,128)(2,1)}, bf16[2,128,1,256]{1,3,2,0:T(8,128)(2,1)S(1)}, u32[]{:S(2)}, u32[]{:S(2)}) collective-permute-start(bf16[2,128,1,256]{1,3,2,0:T(8,128)(2,1)} %get-tuple-element.221), channel_id=1, source_target_pairs={{0,1},{1,2},{2,3},{3,4},{4,5},{5,6},{6,7},{7,8},{8,9},{9,10},{10,1... | collective-permute-start | bytes 393224 | tf_op jit(solution)/shard_map/ppermute | solution.py:18
  214.3 17.7 %copy-start.6 = (s32[1,2]{1,0:T(1,128)S(1)}, s32[1,2]{1,0:T(1,128)}, u32[]{:S(2)}) copy-start(s32[1,2]{1,0:T(1,128)} %param.11) | copy-start | bytes 28
  228.3 31.3 %all-to-all-start.1 = ((bf16[2,2048,1,256]{3,0,2,1:T(2,128)(2,1)}), bf16[2,2048,1,256]{3,0,2,1:T(2,128)(2,1)S(1)}, u32[]{:S(2)}, u32[]{:S(2)}) async-start(bf16[2,2048,1,256]{3,0,2,1:T(2,128)(2,1)} %copy.45), calls=%async_computation.1 | async-start | bytes 4194304 | tf_op jit(solution)/shard_map/all_to_all | solution.py:121
  260.3 26.8 %collective-permute-start.15 = (bf16[2,128,16,256]{3,1,2,0:T(8,128)(2,1)S(1)}, bf16[2,128,16,256]{3,1,2,0:T(8,128)(2,1)}, u32[]{:S(2)}, u32[]{:S(2)}) collective-permute-start(bf16[2,128,16,256]{3,1,2,0:T(8,128)(2,1)S(1)} %pad_maximum_fusion), channel_id=1, source_target_pairs={{112,0},{0,16},{16,32},{32,48},{48,64},{64,80},{80,96},{96,112},{1... | collective-permute-start | bytes 6291464 | tf_op jit(solution)/shard_map/ppermute | solution.py:30
  (16 other events, 77.4 us)
